TPU v7x, 256 devices: a whole 4x4x8 slice. The times are simulated.
256 devices in a mesh: section: 2 (over core), grp: 4 (over x), dev: 32 (over y, z).
Axes of the slice: x: 4, y: 4, z: 8, core: 2. Of those that a mesh axis runs over, the one named last changes fastest.
Arguments:
- frames: bfloat16 [4, 512, 512, 256], P('grp', 'dev', 'section'), may hold values from -6 to 6
- templates: bfloat16 [8192, 256], P('dev'), may hold values from -0.375 to 0.375
- pair_block: int32 [2, 4, 256], P('section', 'grp', 'dev'), may hold values from 0 to 63
- pair_tile: int32 [2, 4, 256], P('section', 'grp', 'dev'), may hold values from 0 to 3
- pair_count: int32 [2, 4, 32], P('section', 'grp', 'dev'), may hold values from 1 to 8, 128 in all within a row
- owner_order: int32 [8192], replicated, may hold values from 0 to 8191, each once
Outputs:
- quantities: float32 [4, 8192], P('grp', 'dev')
Inputs may be any that keep to these rules, and one draw needn't show every extreme that they name: `pair_count`: each device's count of live slots; the counts of one section half and run sum to half of all slots there, and one of them is 8. `owner_order`: A permutation of the precursors.
All inputs are finite; a program needn't handle non-finite values.
Results may differ from a plain program's by a relative error of at most 0.00037.
Values may be sent and summed in bfloat16 or wider, within the bound.
A program may use at most 64 MiB of HBM per device.

v0:
```python
import math
import jax
import jax.numpy as jnp
from jax import lax
from jax.sharding import PartitionSpec as P

MOB = 512
SCALES = 6
RAD = 4
TM = 64
PB = 128
PREC = 8192
retention_spread = 2.0


def extended(cells, sides, width):
    for axis, dim in sides:
        count = lax.axis_size(axis)
        ends = count - 1
        head = lax.slice_in_dim(cells, 0, width, axis=dim)
        tail = lax.slice_in_dim(cells, cells.shape[dim] - width, cells.shape[dim], axis=dim)
        cells = jnp.concatenate(
            [
                lax.ppermute(tail, axis, [(i, (i + 1) % count) for i in range(ends)]),
                cells,
                lax.ppermute(head, axis, [((i + 1) % count, i) for i in range(ends)]),
            ],
            axis=dim,
        )
    return cells


def retention_weights():
    bell_values = [
        math.exp(-0.5 * (offset / retention_spread) ** 2) for offset in range(-RAD, RAD + 1)
    ]
    bell_total = sum(bell_values)
    return [weight_value / bell_total for weight_value in bell_values]


def mobility_kernels(row_start, row_count):
    row_place = (row_start + jnp.arange(row_count, dtype=jnp.int32)).astype(jnp.float32)
    col_place = jnp.arange(MOB, dtype=jnp.int32).astype(jnp.float32)
    distance = row_place[:, None] - col_place[None, :]
    tables = []
    for level in range(SCALES):
        spread_scans = 2.0**level
        scaled = distance / spread_scans
        tables.append(
            (1.0 - scaled * scaled)
            * jnp.exp(-0.5 * scaled * scaled)
            / math.sqrt(0.75 * math.sqrt(math.pi) * spread_scans)
        )
    return jnp.stack(tables).astype(jnp.bfloat16)


def on_device(frames, templates, pair_block, pair_tile, pair_count, owner_order):
    section_index = lax.axis_index("section")
    weights = retention_weights()
    count_frames = frames.shape[1]
    mob_local = frames.shape[2]
    channels = frames.shape[3]
    framed = extended(frames, (("dev", 1),), RAD)
    padded = framed.astype(jnp.float32)
    smoothed = weights[0] * padded[:, 0:count_frames]
    for offset in range(1, 2 * RAD + 1):
        smoothed = smoothed + weights[offset] * padded[:, offset : offset + count_frames]
    smoothed = smoothed.astype(jnp.bfloat16)
    gathered = lax.all_gather(smoothed, "section", axis=2, tiled=True)
    kernels = mobility_kernels(section_index * mob_local, mob_local)
    wavelet_stack = jnp.einsum(
        "smn,fnc->smfc", kernels, gathered[0], preferred_element_type=jnp.float32
    ).astype(jnp.bfloat16)
    template_panel = lax.all_gather(templates, "dev", axis=0, tiled=True)
    blocks = template_panel.shape[0] // PB
    live_pairs = pair_count[0, 0, 0]
    block_ids = pair_block[0, 0]
    tile_ids = pair_tile[0, 0]

    def visit_pair(slot_index, totals):
        block_id = block_ids[slot_index]
        tile_id = tile_ids[slot_index]
        tile_cells = lax.dynamic_slice_in_dim(wavelet_stack, tile_id * TM, TM, 1).reshape(
            -1, channels
        )
        block_rows = lax.dynamic_slice_in_dim(template_panel, block_id * PB, PB, 0)
        scores = jnp.dot(tile_cells, block_rows.T, preferred_element_type=jnp.float32)
        response = jnp.mean(jnp.maximum(scores, 0.0), axis=0)
        block_hit = (jnp.arange(blocks, dtype=jnp.int32) == block_id).astype(jnp.float32)
        return totals + block_hit[:, None] * response[None, :]

    totals = lax.fori_loop(0, live_pairs, visit_pair, jnp.zeros((blocks, PB), jnp.float32))
    placed = jnp.zeros((PREC,), jnp.float32).at[owner_order].set(totals.reshape(-1))[None]
    summed = lax.psum(placed, "section")
    owned = lax.psum_scatter(summed, "dev", scatter_dimension=1, tiled=True)
    run_count = lax.axis_size("grp")
    run_mask = (jnp.arange(run_count, dtype=jnp.int32) == lax.axis_index("grp")).astype(jnp.float32)
    run_totals = lax.psum(run_mask * jnp.sum(owned), ("grp", "dev"))
    own_total = jnp.sum(run_totals * run_mask)
    factor = jnp.mean(run_totals) / own_total
    return owned * factor


def solution(mesh):
    placed = (
        P("grp", "dev", "section", None),
        P("dev", None),
        P("section", "grp", "dev"),
        P("section", "grp", "dev"),
        P("section", "grp", "dev"),
        P(),
    )
    return jax.shard_map(
        on_device, mesh=mesh, in_specs=placed, out_specs=P("grp", "dev"), check_vma=False
    )
```

profile of v0, /device:TPU:0, one launch (start us, length us, event | category | flops | bytes accessed | tf_op | source)
XLA Modules:
  0.0 833.9 jit_solution(16655650894832102042)
XLA Ops:
  6.5 0.0 all-gather.3.cloned.1.call-start
  6.5 1.3 fusion.63
  7.8 2.1 collective-permute-start
  9.9 1.3 collective-permute-start.1
  11.2 9.8 %collective-permute-done = bf16[1,4,256,256]{3,2,1,0:T(8,128)(2,1)S(1)} collective-permute-done((bf16[1,4,256,256]{3,2,1,0:T(8,128)(2,1)S(1)}, bf16[1,4,256,256]{3,2,1,0:T(8,128)(2,1)S(1)}, u32[]{:S(2)}, u32[]{:S(2)}) %collective-permute-start) | collective-permute-done | bytes 524320 | tf_op jit(solution)/shard_map/ppermute | solution.py:24
  21.1 4.3 collective-permute-done.1
  25.4 2.1 maximum_convert_fusion
  27.4 0.0 copy-start
  27.4 5.7 fusion.4
  33.1 0.0 all-gather.3.cloned.1.call-update
  33.2 0.0 all-gather.5.cloned.1.call-start
  33.2 0.7 all-gather.5.cloned.1.call-update
  33.9 0.0 reduce-scatter.4.cloned.1.call-start
  34.0 0.0 copy-done
  34.0 0.2 fusion.59
  34.3 0.3 fusion.54
  34.5 0.3 fusion.55
  34.8 0.3 fusion.56
  35.0 0.3 fusion.57
  35.3 0.3 fusion.58
  35.5 0.0 copy-start.1
  35.6 0.0 copy-start.2
  35.6 19.7 %all-gather.3.cloned.1.call-done = bf16[1,16,512,256]{3,2,1,0:T(8,128)(2,1)} async-done(((bf16[1,16,256,256]{3,2,1,0:T(8,128)(2,1)}), bf16[1,16,512,256]{3,2,1,0:T(8,128)(2,1)}) %all-gather.3.cloned.1.call-update) | async-done | bytes 4194320 | tf_op jit(solution)/shard_map/all_gather | solution.py:69
  55.2 11.7 %convolution_convert_fusion = bf16[6,256,16,256]{3,1,2,0:T(8,128)(2,1)} fusion(bf16[1,16,512,256]{3,2,1,0:T(8,128)(2,1)} %all-gather.3.cloned.1.call-done, bf16[6,256,512]{2,1,0:T(8,128)(2,1)S(1)} %fusion.58), kind=kOutput, calls=%fused_computation.9 | convolution fusion | flops 6448742400 | bytes 18350080 | tf_op jit(solution)/shard_map/smn,fnc->smfc/dot_general | solution.py:71
  66.9 73.7 %all-gather.5.cloned.1.call-done = bf16[8192,256]{1,0:T(8,128)(2,1)} async-done(((bf16[256,256]{1,0:T(8,128)(2,1)}), bf16[8192,256]{1,0:T(8,128)(2,1)}) %all-gather.5.cloned.1.call-update) | async-done | bytes 4194320 | tf_op jit(solution)/shard_map/all_gather | solution.py:74
  140.7 0.0 copy-done.1
  140.7 0.0 copy-done.2
  140.7 10.7 %while.10 = (s32[]{:T(128)}, f32[64,128]{1,0:T(8,128)S(1)}, s32[]{:T(128)}, s32[8]{0:T(128)S(1)}, s32[8]{0:T(128)S(1)}, /*index=5*/bf16[6,256,16,256]{3,1,2,0:T(...) while((s32[]{:T(128)}, f32[64,128]{1,0:T(8,128)S(1)}, ...), condition=%wide.region_2.0_spmd, body=%wide.region_0.0_spmd.sunk | while | flops 404242560 | bytes 15862567 | solution.py:92
  141.4 0.6 dynamic_slice.21
  142.5 2.3 constant_dynamic-slice_fusion.2
  144.8 1.9 copy.14
  146.7 0.6 dynamic_slice.22
  147.9 2.2 fusion.70
  150.1 0.6 compare_convert_fusion.2
  150.7 0.1 multiply_add_fusion.2
  151.4 30.5 %scatter_custom_fusion = f32[8192]{0:T(1024)S(1)} fusion(s32[8192]{0:T(1024)S(1)} %compare_select_fusion, f32[8192]{0:T(1024)S(1)} %bitcast.30, f32[]{:T(128)} %constant.32.clone.1), kind=kCustom, calls=%fused_computation.91 | custom fusion | bytes 32772 | tf_op jit(solution)/shard_map/scatter | solution.py:93
  181.9 2.6 copy.10
  184.5 0.0 reduce-scatter.4.cloned.1.call-update
  184.6 288.7 %reduce-scatter.4.cloned.1.call-done = f32[256,1]{1,0:T(8,128)} async-done(((f32[8192,1]{1,0:T(8,128)}), f32[256,1]{1,0:T(8,128)}) %reduce-scatter.4.cloned.1.call-update) | async-done | bytes 1040
  473.2 1.0 copy.11
  474.2 2.5 psum.16
  476.7 0.6 reduce_sum.36
  477.3 0.6 compare_select_fusion.2
  477.9 346.8 %psum.15 = f32[4]{0:T(128)S(1)} all-reduce(f32[4]{0:T(128)S(1)} %compare_select_fusion.2), channel_id=1, replica_groups=mesh['section'=2,'grp'=4,'dev'=32] {'grp','dev'}, use_global_device_ids=true, to_apply=%region_7.0 | all-reduce | flops 4 | bytes 32 | tf_op jit(solution)/shard_map/psum | solution.py:98
  824.8 0.7 fusion.62
  826.8 0.6 broadcast_multiply_fusion.1
  (5 shorter events, 0.0 us)
Async XLA Ops:
  6.5 48.7 %all-gather.3.cloned.1.call-start = ((), (), s32[]{:S(2)}) async-start(), calls=%async_computation.1 | async-start | bytes 6291456 | tf_op jit(solution)/shard_map/all_gather | solution.py:69
  7.8 13.3 %collective-permute-start = (bf16[1,4,256,256]{3,2,1,0:T(8,128)(2,1)S(1)}, bf16[1,4,256,256]{3,2,1,0:T(8,128)(2,1)S(1)}, u32[]{:S(2)}, u32[]{:S(2)}) collective-permute-start(bf16[1,4,256,256]{3,2,1,0:T(8,128)(2,1)S(1)} %get-tuple-element.74), channel_id=1, source_target_pairs={{0,1},{1,2},{2,3},{3,4},{4,5},{5,6},{6,7},{7,8},{8,9},{9,10},{10,1... | collective-permute-start | bytes 1572872 | tf_op jit(solution)/shard_map/ppermute | solution.py:24
  9.9 15.4 %collective-permute-start.1 = (bf16[1,4,256,256]{3,2,1,0:T(8,128)(2,1)S(1)}, bf16[1,4,256,256]{3,2,1,0:T(8,128)(2,1)S(1)}, u32[]{:S(2)}, u32[]{:S(2)}) collective-permute-start(bf16[1,4,256,256]{3,2,1,0:T(8,128)(2,1)S(1)} %get-tuple-element.75), channel_id=1, source_target_pairs={{1,0},{2,1},{3,2},{4,3},{5,4},{6,5},{7,6},{8,7},{9,8},{10,9},{11,1... | collective-permute-start | bytes 1572872 | tf_op jit(solution)/shard_map/ppermute | solution.py:26
  27.4 6.6 copy-start
  33.2 107.5 %all-gather.5.cloned.1.call-start = ((), (), s32[]{:S(2)}) async-start(), calls=%async_computation.2 | async-start | bytes 4325376 | tf_op jit(solution)/shard_map/all_gather | solution.py:74
  33.9 439.3 %reduce-scatter.4.cloned.1.call-start = ((), (), s32[]{:S(2)}) async-start(), calls=%async_computation.3 | async-start | bytes 4325376
  35.5 105.1 %copy-start.1 = (s32[1,1,8]{2,1,0:T(1,128)S(1)}, s32[1,1,8]{2,1,0:T(1,128)}, u32[]{:S(2)}) copy-start(s32[1,1,8]{2,1,0:T(1,128)} %param.10) | copy-start | bytes 100
  35.6 105.1 %copy-start.2 = (s32[1,1,8]{2,1,0:T(1,128)S(1)}, s32[1,1,8]{2,1,0:T(1,128)}, u32[]{:S(2)}) copy-start(s32[1,1,8]{2,1,0:T(1,128)} %param.11) | copy-start | bytes 100
Sparse Core Ops, SparseCore 0:
  33.3 21.9 all-gather.2
  57.8 82.8 all-gather.4
  184.7 288.5 reduce-scatter.3
where the time goes:
time: 835 us; the launch traced here: 834 us
  waiting for transfers between devices  397 us (48%)
  blocking collectives  349 us (42%)
  local copies, waits for them, and re-layouts  40.7 us (5%)
  between operations  14.6 us (2%)
  matrix products  13.9 us (2%)
  other arithmetic  12.4 us (1%)
    psum x1, blocking collectives, on_device(): run_totals = lax.psum(run_mask * jnp.sum(owned), ('grp', 'dev'))  347 us
    unnamed x4, waiting for transfers between devices  289 us
    all_gather x1, waiting for transfers between devices, on_device(): template_panel = lax.all_gather(templates, 'dev', axis=0, tiled=True)  73.7 us
    scatter x1, local copies, waits for them, and re-layouts, on_device(): jnp.zeros((PREC,), jnp.float32).at[owner_order].set(totals.reshape(-1))  30.5 us
    all_gather x1, waiting for transfers between devices, on_device(): gathered = lax.all_gather(smoothed, 'section', axis=2, tiled=True)  19.7 us
  transfers between devices with their start and end apart: 5, of which 5 were waited for; matrix products, arithmetic and copies ran while one was open for 2% of the time, Pallas kernels for 0%

commit v1 on v0

--- a/solution.py
+++ b/solution.py
@@ -95,7 +95,7 @@
     owned = lax.psum_scatter(summed, "dev", scatter_dimension=1, tiled=True)
     run_count = lax.axis_size("grp")
     run_mask = (jnp.arange(run_count, dtype=jnp.int32) == lax.axis_index("grp")).astype(jnp.float32)
-    run_totals = lax.psum(run_mask * jnp.sum(owned), ("grp", "dev"))
+    run_totals = lax.psum(lax.psum(run_mask * jnp.sum(owned), "grp"), "dev")
     own_total = jnp.sum(run_totals * run_mask)
     factor = jnp.mean(run_totals) / own_total
     return owned * factor

time: 835 us -> 571 us (0.68)
  blocking collectives: 349 us -> 85.1 us
    psum x1 -> x2, blocking collectives: 347 us -> 82.6 us  [on_device(): run_totals = lax.psum(lax.psum(run_mask * jnp.sum(owned), 'grp'), 'dev')]
where the time goes in v1:
time: 571 us; the launch traced here: 570 us
  waiting for transfers between devices  397 us (70%)
  blocking collectives  85.1 us (15%)
  local copies, waits for them, and re-layouts  40.7 us (7%)
  between operations  14.6 us (3%)
  matrix products  13.9 us (2%)
  other arithmetic  12.4 us (2%)
    unnamed x4, waiting for transfers between devices  289 us
    psum x2, blocking collectives, on_device(): run_totals = lax.psum(lax.psum(run_mask * jnp.sum(owned), 'grp'), 'dev')  82.6 us
    all_gather x1, waiting for transfers between devices, on_device(): template_panel = lax.all_gather(templates, 'dev', axis=0, tiled=True)  73.7 us
    scatter x1, local copies, waits for them, and re-layouts, on_device(): jnp.zeros((PREC,), jnp.float32).at[owner_order].set(totals.reshape(-1))  30.5 us
    all_gather x1, waiting for transfers between devices, on_device(): gathered = lax.all_gather(smoothed, 'section', axis=2, tiled=True)  19.7 us
    dot_general x1, matrix products, on_device(): jnp.einsum('smn,fnc->smfc', kernels, gathered[0], preferred_element_type=...  11.7 us
  transfers between devices with their start and end apart: 5, of which 5 were waited for; matrix products, arithmetic and copies ran while one was open for 2% of the time, Pallas kernels for 0%

profile of v1, /device:TPU:0, one launch (start us, length us, event | category | flops | bytes accessed | tf_op | source)
XLA Modules:
  0.0 569.7 jit_solution(2481325818425955099)
XLA Ops:
  6.5 0.0 all-gather.3.cloned.1.call-start
  6.5 1.3 fusion.63
  7.8 2.1 collective-permute-start
  9.9 1.3 collective-permute-start.1
  11.2 9.8 %collective-permute-done = bf16[1,4,256,256]{3,2,1,0:T(8,128)(2,1)S(1)} collective-permute-done((bf16[1,4,256,256]{3,2,1,0:T(8,128)(2,1)S(1)}, bf16[1,4,256,256]{3,2,1,0:T(8,128)(2,1)S(1)}, u32[]{:S(2)}, u32[]{:S(2)}) %collective-permute-start) | collective-permute-done | bytes 524320 | tf_op jit(solution)/shard_map/ppermute | solution.py:24
  21.1 4.3 collective-permute-done.1
  25.4 2.1 maximum_convert_fusion
  27.4 0.0 copy-start
  27.4 5.7 %fusion.4 = bf16[1,16,256,256]{3,2,1,0:T(8,128)(2,1)} fusion(f32[1,24,256,256]{3,2,1,0:T(8,128)S(1)} %maximum_convert_fusion), kind=kLoop, calls=%fused_computation.12 | loop fusion | flops 18874368 | bytes 39845888 | tf_op jit(solution)/shard_map/convert_element_type | solution.py:68
  33.1 0.0 all-gather.3.cloned.1.call-update
  33.2 0.0 all-gather.5.cloned.1.call-start
  33.2 0.7 all-gather.5.cloned.1.call-update
  33.9 0.0 reduce-scatter.4.cloned.1.call-start
  34.0 0.0 copy-done
  34.0 0.2 fusion.59
  34.3 0.3 fusion.54
  34.5 0.3 fusion.55
  34.8 0.3 fusion.56
  35.0 0.3 fusion.57
  35.3 0.3 fusion.58
  35.5 0.0 copy-start.1
  35.6 0.0 copy-start.2
  35.6 19.7 %all-gather.3.cloned.1.call-done = bf16[1,16,512,256]{3,2,1,0:T(8,128)(2,1)} async-done(((bf16[1,16,256,256]{3,2,1,0:T(8,128)(2,1)}), bf16[1,16,512,256]{3,2,1,0:T(8,128)(2,1)}) %all-gather.3.cloned.1.call-update) | async-done | bytes 4194320 | tf_op jit(solution)/shard_map/all_gather | solution.py:69
  55.2 11.7 %convolution_convert_fusion = bf16[6,256,16,256]{3,1,2,0:T(8,128)(2,1)} fusion(bf16[1,16,512,256]{3,2,1,0:T(8,128)(2,1)} %all-gather.3.cloned.1.call-done, bf16[6,256,512]{2,1,0:T(8,128)(2,1)S(1)} %fusion.58), kind=kOutput, calls=%fused_computation.9 | convolution fusion | flops 6448742400 | bytes 18350080 | tf_op jit(solution)/shard_map/smn,fnc->smfc/dot_general | solution.py:71
  66.9 73.7 %all-gather.5.cloned.1.call-done = bf16[8192,256]{1,0:T(8,128)(2,1)} async-done(((bf16[256,256]{1,0:T(8,128)(2,1)}), bf16[8192,256]{1,0:T(8,128)(2,1)}) %all-gather.5.cloned.1.call-update) | async-done | bytes 4194320 | tf_op jit(solution)/shard_map/all_gather | solution.py:74
  140.7 0.0 copy-done.1
  140.7 0.0 copy-done.2
  140.7 10.7 %while.10 = (s32[]{:T(128)}, f32[64,128]{1,0:T(8,128)S(1)}, s32[]{:T(128)}, s32[8]{0:T(128)S(1)}, s32[8]{0:T(128)S(1)}, /*index=5*/bf16[6,256,16,256]{3,1,2,0:T(...) while((s32[]{:T(128)}, f32[64,128]{1,0:T(8,128)S(1)}, ...), condition=%wide.region_2.0_spmd, body=%wide.region_0.0_spmd.sunk | while | flops 404242560 | bytes 15862567 | solution.py:92
  141.4 0.6 dynamic_slice.21
  142.5 2.3 constant_dynamic-slice_fusion.2
  144.8 1.9 copy.14
  146.7 0.6 dynamic_slice.22
  147.9 2.2 fusion.70
  150.1 0.6 compare_convert_fusion.2
  150.7 0.1 multiply_add_fusion.2
  151.4 30.5 %scatter_custom_fusion = f32[8192]{0:T(1024)S(1)} fusion(s32[8192]{0:T(1024)S(1)} %compare_select_fusion, f32[8192]{0:T(1024)S(1)} %bitcast.30, f32[]{:T(128)} %constant.32.clone.1), kind=kCustom, calls=%fused_computation.91 | custom fusion | bytes 32772 | tf_op jit(solution)/shard_map/scatter | solution.py:93
  181.9 2.6 copy.10
  184.5 0.0 reduce-scatter.4.cloned.1.call-update
  184.6 288.7 %reduce-scatter.4.cloned.1.call-done = f32[256,1]{1,0:T(8,128)} async-done(((f32[8192,1]{1,0:T(8,128)}), f32[256,1]{1,0:T(8,128)}) %reduce-scatter.4.cloned.1.call-update) | async-done | bytes 1040
  473.2 1.0 copy.11
  474.2 2.5 psum.24
  476.7 0.6 reduce_sum.36
  477.3 0.6 compare_select_fusion.2
  477.9 10.4 %psum.22 = f32[4]{0:T(128)S(1)} all-reduce(f32[4]{0:T(128)S(1)} %compare_select_fusion.2), channel_id=1, replica_groups=mesh['section'=2,'grp'=4,'dev'=32] {'grp'}, use_global_device_ids=true, to_apply=%region_7.0 | all-reduce | flops 4 | bytes 32 | tf_op jit(solution)/shard_map/psum | solution.py:98
  488.4 72.2 %psum.23 = f32[4]{0:T(128)S(1)} all-reduce(f32[4]{0:T(128)S(1)} %psum.22), channel_id=1, replica_groups=mesh['section'=2,'grp'=4,'dev'=32] {'dev'}, use_global_device_ids=true, to_apply=%region_8.0 | all-reduce | flops 4 | bytes 32 | tf_op jit(solution)/shard_map/psum | solution.py:98
  560.5 0.7 fusion.62
  562.6 0.6 broadcast_multiply_fusion.1
  (5 shorter events, 0.0 us)
Async XLA Ops:
  6.5 48.7 %all-gather.3.cloned.1.call-start = ((), (), s32[]{:S(2)}) async-start(), calls=%async_computation.1 | async-start | bytes 6291456 | tf_op jit(solution)/shard_map/all_gather | solution.py:69
  7.8 13.3 %collective-permute-start = (bf16[1,4,256,256]{3,2,1,0:T(8,128)(2,1)S(1)}, bf16[1,4,256,256]{3,2,1,0:T(8,128)(2,1)S(1)}, u32[]{:S(2)}, u32[]{:S(2)}) collective-permute-start(bf16[1,4,256,256]{3,2,1,0:T(8,128)(2,1)S(1)} %get-tuple-element.74), channel_id=1, source_target_pairs={{0,1},{1,2},{2,3},{3,4},{4,5},{5,6},{6,7},{7,8},{8,9},{9,10},{10,1... | collective-permute-start | bytes 1572872 | tf_op jit(solution)/shard_map/ppermute | solution.py:24
  9.9 15.4 %collective-permute-start.1 = (bf16[1,4,256,256]{3,2,1,0:T(8,128)(2,1)S(1)}, bf16[1,4,256,256]{3,2,1,0:T(8,128)(2,1)S(1)}, u32[]{:S(2)}, u32[]{:S(2)}) collective-permute-start(bf16[1,4,256,256]{3,2,1,0:T(8,128)(2,1)S(1)} %get-tuple-element.75), channel_id=1, source_target_pairs={{1,0},{2,1},{3,2},{4,3},{5,4},{6,5},{7,6},{8,7},{9,8},{10,9},{11,1... | collective-permute-start | bytes 1572872 | tf_op jit(solution)/shard_map/ppermute | solution.py:26
  27.4 6.6 %copy-start = (s32[8192]{0:T(1024)S(1)}, s32[8192]{0:T(1024)}, u32[]{:S(2)}) copy-start(s32[8192]{0:T(1024)} %param.13) | copy-start | bytes 98308
  33.2 107.5 %all-gather.5.cloned.1.call-start = ((), (), s32[]{:S(2)}) async-start(), calls=%async_computation.2 | async-start | bytes 4325376 | tf_op jit(solution)/shard_map/all_gather | solution.py:74
  33.9 439.3 %reduce-scatter.4.cloned.1.call-start = ((), (), s32[]{:S(2)}) async-start(), calls=%async_computation.3 | async-start | bytes 4325376
  35.5 105.1 %copy-start.1 = (s32[1,1,8]{2,1,0:T(1,128)S(1)}, s32[1,1,8]{2,1,0:T(1,128)}, u32[]{:S(2)}) copy-start(s32[1,1,8]{2,1,0:T(1,128)} %param.10) | copy-start | bytes 100
  35.6 105.1 %copy-start.2 = (s32[1,1,8]{2,1,0:T(1,128)S(1)}, s32[1,1,8]{2,1,0:T(1,128)}, u32[]{:S(2)}) copy-start(s32[1,1,8]{2,1,0:T(1,128)} %param.11) | copy-start | bytes 100
Sparse Core Ops, SparseCore 0:
  33.3 21.9 all-gather.2
  57.8 82.8 all-gather.4
  184.7 288.5 reduce-scatter.3
